TPU v7x, 32 devices: a whole 2x2x4 slice. The times are simulated.
32 devices in a mesh: groups: 2 (over x), wide: 16 (over z, y, core).
Axes of the slice: x: 2, y: 2, z: 4, core: 2. Of those that a mesh axis runs over, the one named last changes fastest.
Arguments:
- queries: bfloat16 [128, 16, 1024], P(('groups', 'wide')), parts along dimension 0, may hold values from -6.5 to 6.5
- cache_keys: bfloat16 [128, 1024, 128], P(('groups', 'wide')), parts along dimension 0, may hold values from -6.5 to 6.5
- cache_values: bfloat16 [128, 1024, 128], P(('groups', 'wide')), parts along dimension 0, may hold values from -32 to 32
- new_keys: bfloat16 [128, 16, 128], P(('groups', 'wide')), parts along dimension 0, may hold values from -15 to 15
- new_values: bfloat16 [128, 16, 128], P(('groups', 'wide')), parts along dimension 0, may hold values from -32 to 32
- cache_lengths: int32 [16], P('groups'), parts along dimension 0, may hold values from 64 to 1024, as said below
- step_segments: int32 [16, 16], P('groups'), parts along dimension 0, may hold values from 0 to 3, never falling along the last dimension, each value on 1 to 8 neighbouring positions
- resid_in: bfloat16 [256, 8192], P('groups', 'wide'), parts along dimension 0, may hold values from -70 to 70
- out_weight: bfloat16 [8192, 8192], P(None, 'wide'), may hold values from -0.0625 to 0.0625
- norm_gain: float32 [8192], replicated, may hold values from 0.1 to 1.9
- gate_weight: bfloat16 [8192, 16384], P(None, 'wide'), may hold values from -0.0625 to 0.0625
- up_weight: bfloat16 [8192, 16384], P(None, 'wide'), may hold values from -0.0625 to 0.0625
Outputs:
- residual: bfloat16 [256, 8192], P('groups', 'wide'), parts along dimension 0
- activ: bfloat16 [256, 16384], P('groups', 'wide'), parts along dimension 0
There are 2 independent parts, one for each index of `groups`. A program takes and returns all parts, laid end to end along the dimension named above; an argument that names none is the same for every part. Nothing has to cross between parts.
Inputs may be any that keep to these rules, and one draw needn't show every extreme that they name: `cache_lengths`: some beam has all 1024 slots live. `step_segments`: never falling along a beam's steps.
All inputs are finite; a program needn't handle non-finite values.
Results may differ from a plain program's by a relative error of at most 0.0082.
Values may be sent and summed in bfloat16 or wider, within the bound.
No kernel may reach another device: no remote copies, remote signals or barrier semaphores. Data moves between devices by JAX's collectives and lax.ppermute only.
A program may use at most 128 MiB of HBM per device.

v0:
```python
import math

import jax
import jax.numpy as jnp
from jax import lax
from jax.sharding import PartitionSpec as P

D = 8192


def attend(queries, cache_keys, cache_values, new_keys, new_values, cache_lengths, step_segments):
    pair_count, step_count, width = queries.shape
    slot_count, head_dim = (cache_keys.shape[1], cache_keys.shape[2])
    beam_count = cache_lengths.shape[0]
    first_pair = lax.axis_index("wide") * pair_count
    beam_ids = (first_pair + jnp.arange(pair_count, dtype=jnp.int32)) % beam_count
    onehot = (beam_ids[:, None] == jnp.arange(beam_count, dtype=jnp.int32)[None, :]).astype(
        jnp.int32
    )
    live_length = jnp.sum(onehot * cache_lengths[None, :], axis=1)
    segment_ids = jnp.sum(onehot[:, :, None] * step_segments[None, :, :], axis=1)
    query_heads = queries.reshape(pair_count, step_count, width // head_dim, head_dim)
    score_scale = 1.0 / math.sqrt(head_dim)
    old_scores = (
        jnp.einsum("psgd,pkd->psgk", query_heads, cache_keys, preferred_element_type=jnp.float32)
        * score_scale
    )
    new_scores = (
        jnp.einsum("psgd,pjd->psgj", query_heads, new_keys, preferred_element_type=jnp.float32)
        * score_scale
    )
    slot_pos = jnp.arange(slot_count, dtype=jnp.int32)
    old_live = slot_pos[None, :] < live_length[:, None]
    step_pos = jnp.arange(step_count, dtype=jnp.int32)
    same_segment = segment_ids[:, None, :] == segment_ids[:, :, None]
    new_live = same_segment & (step_pos[None, None, :] <= step_pos[None, :, None])
    old_scores = jnp.where(old_live[:, None, None, :], old_scores, -jnp.inf)
    new_scores = jnp.where(new_live[:, :, None, :], new_scores, -jnp.inf)
    row_max = jnp.maximum(
        jnp.max(old_scores, axis=3, keepdims=True), jnp.max(new_scores, axis=3, keepdims=True)
    )
    old_expon = jnp.exp(old_scores - row_max)
    new_expon = jnp.exp(new_scores - row_max)
    denom = jnp.sum(old_expon, axis=3, keepdims=True) + jnp.sum(new_expon, axis=3, keepdims=True)
    old_weights = (old_expon / denom).astype(jnp.bfloat16)
    new_weights = (new_expon / denom).astype(jnp.bfloat16)
    mixed = jnp.einsum(
        "psgk,pkd->psgd", old_weights, cache_values, preferred_element_type=jnp.float32
    )
    mixed = mixed + jnp.einsum(
        "psgj,pjd->psgd", new_weights, new_values, preferred_element_type=jnp.float32
    )
    return mixed.astype(jnp.bfloat16).reshape(pair_count, step_count, width)


def per_device(
    queries,
    cache_keys,
    cache_values,
    new_keys,
    new_values,
    cache_lengths,
    step_segments,
    resid_in,
    out_weight,
    norm_gain,
    gate_weight,
    up_weight,
):
    attention = attend(
        queries, cache_keys, cache_values, new_keys, new_values, cache_lengths, step_segments
    )
    width = attention.shape[2]
    col_count = out_weight.shape[1]
    group_count = out_weight.shape[0] // width
    gathered = lax.all_gather(attention, "wide", axis=0, tiled=True)
    stacked = gathered.reshape(group_count, -1, width)
    projected = jnp.einsum(
        "gtj,gjc->tc",
        stacked,
        out_weight.reshape(group_count, width, col_count),
        preferred_element_type=jnp.float32,
    )
    residual = (resid_in.astype(jnp.float32) + projected).astype(jnp.bfloat16)
    whole = lax.all_gather(residual, "wide", axis=1, tiled=True)
    wide_rows = whole.astype(jnp.float32)
    inverse = lax.rsqrt(jnp.sum(wide_rows * wide_rows, axis=1) / D + 1e-06)
    normed = (wide_rows * inverse[:, None] * norm_gain[None, :]).astype(jnp.bfloat16)
    gate = jnp.dot(normed, gate_weight, preferred_element_type=jnp.float32)
    up_part = jnp.dot(normed, up_weight, preferred_element_type=jnp.float32)
    activ = (jax.nn.silu(gate) * up_part).astype(jnp.bfloat16)
    return (residual, activ)


def solution(mesh):
    placed = (
        P(("groups", "wide"), None, None),
        P(("groups", "wide"), None, None),
        P(("groups", "wide"), None, None),
        P(("groups", "wide"), None, None),
        P(("groups", "wide"), None, None),
        P("groups"),
        P("groups", None),
        P("groups", "wide"),
        P(None, "wide"),
        P(),
        P(None, "wide"),
        P(None, "wide"),
    )
    return jax.shard_map(
        per_device,
        mesh=mesh,
        in_specs=placed,
        out_specs=(P("groups", "wide"), P("groups", "wide")),
        check_vma=False,
    )
```

profile of v0, /device:TPU:0, one launch (start us, length us, event | category | flops | bytes accessed | tf_op | source)
XLA Modules:
  0.0 131.3 jit_solution(3958309878773686089)
XLA Ops:
  7.2 0.0 copy-start
  7.2 0.0 all-gather.3.cloned.1.call-start
  7.3 0.1 fusion.25
  7.3 0.9 select_reduce_fusion
  8.3 0.1 iota_compare_fusion
  8.3 0.9 copy.18
  9.3 0.8 multiply_reduce_fusion
  10.0 0.1 compare_and_fusion
  10.1 1.0 fusion.29
  11.1 0.0 copy-done
  11.1 0.5 fusion.3
  11.7 0.0 copy-start.3
  11.7 0.3 fusion.18
  12.0 0.6 fusion.4
  12.5 0.4 copy-done.3
  12.9 0.0 copy-start.5
  12.9 0.0 copy-start.2
  12.9 0.7 fusion.10
  13.6 0.0 copy-done.5
  13.6 0.3 fusion.9
  13.9 0.7 reshape.109
  14.7 0.0 all-gather.3.cloned.1.call-update
  14.7 0.0 all-gather.5.cloned.1.call-start
  14.7 44.3 %all-gather.3.cloned.1.call-done = bf16[64,16,1024]{2,1,0:T(8,128)(2,1)} async-done(((bf16[4,16,1024]{2,1,0:T(8,128)(2,1)}), bf16[64,16,1024]{2,1,0:T(8,128)(2,1)}) %all-gather.3.cloned.1.call-update) | async-done | bytes 2097168 | tf_op jit(solution)/shard_map/all_gather | solution.py:76
  59.0 0.0 copy-done.2
  59.0 5.9 %fusion.8 = bf16[128,512]{1,0:T(8,128)(2,1)} fusion(bf16[8,128,1024]{2,1,0:T(8,128)(2,1)} %bitcast.55, bf16[8,1024,512]{2,1,0:T(8,128)(2,1)} %bitcast.54, bf16[128,512]{1,0:T(8,128)(2,1)S(1)} %copy-done.2), kind=kOutput, calls=%fused_computation.17 | convolution fusion | flops 1073938432 | bytes 10747904 | tf_op jit(solution)/shard_map/gtj,gjc->tc/dot_general | solution.py:78
  65.0 0.0 copy-start.4
  65.0 0.0 all-gather.5.cloned.1.call-update
  65.0 39.9 %all-gather.5.cloned.1.call-done = bf16[128,8192]{1,0:T(8,128)(2,1)} async-done(((bf16[128,512]{1,0:T(8,128)(2,1)}), bf16[128,8192]{1,0:T(8,128)(2,1)}) %all-gather.5.cloned.1.call-update) | async-done | bytes 2097168 | tf_op jit(solution)/shard_map/all_gather | solution.py:85
  104.9 0.0 copy-start.1
  104.9 2.2 %fusion = f32[128]{0:T(128)S(1)} fusion(bf16[128,8192]{1,0:T(8,128)(2,1)} %all-gather.5.cloned.1.call-done), kind=kLoop, calls=%fused_computation.2 | loop fusion | flops 3145600 | bytes 2097664 | tf_op jit(solution)/shard_map/reduce_sum | solution.py:87
  107.1 0.0 copy-done.4
  107.1 0.0 copy-done.1
  107.2 8.3 %fusion.16 = f32[128,1024]{1,0:T(8,128)S(1)} fusion(bf16[8192,1024]{1,0:T(8,128)(2,1)} %param.22, bf16[128,8192]{1,0:T(8,128)(2,1)S(1)} %copy-done.1, f32[8192]{0:T(1024)S(1)} %copy-done.4, f32[128]{0:T(128)S(1)} %add_rsqrt_fusion), kind=kOutput, calls=%fused_computation.24 | convolution fusion | flops 2151677952 | bytes 19431936 | tf_op jit(solution)/shard_map/dot_general | solution.py:89
  115.4 9.0 %fusion.5 = bf16[128,1024]{1,0:T(8,128)(2,1)} fusion(bf16[8192,1024]{1,0:T(8,128)(2,1)} %param.23, bf16[128,8192]{1,0:T(8,128)(2,1)S(1)} %copy-done.1, f32[8192]{0:T(1024)S(1)} %copy-done.4, f32[128]{0:T(128)S(1)} %add_rsqrt_fusion, f32[128,1024]{1,0:T(8,128)S(1)} %fusion.16), kind=kOutput, calls=%fused_computation.11 | convolution fusion | flops 2152464384 | bytes 19694080 | tf_op jit(solution)/shard_map/dot_general | solution.py:90
  (5 shorter events, 0.0 us)
Async XLA Ops:
  7.2 4.0 %copy-start = (bf16[4,1024,128]{2,1,0:T(8,128)(2,1)S(1)}, bf16[4,1024,128]{2,1,0:T(8,128)(2,1)}, u32[]{:S(2)}) copy-start(bf16[4,1024,128]{2,1,0:T(8,128)(2,1)} %param.13) | copy-start | bytes 3145732
  7.2 51.8 %all-gather.3.cloned.1.call-start = ((), (), s32[]{:S(2)}) async-start(), calls=%async_computation | async-start | bytes 2228224 | tf_op jit(solution)/shard_map/all_gather | solution.py:76
  11.7 1.2 copy-start.3
  12.9 0.7 copy-start.5
  12.9 46.1 %copy-start.2 = (bf16[128,512]{1,0:T(8,128)(2,1)S(1)}, bf16[128,512]{1,0:T(8,128)(2,1)}, u32[]{:S(2)}) copy-start(bf16[128,512]{1,0:T(8,128)(2,1)} %param.19) | copy-start | bytes 393220
  14.7 90.2 %all-gather.5.cloned.1.call-start = ((), (), s32[]{:S(2)}) async-start(), calls=%async_computation.1 | async-start | bytes 2228224 | tf_op jit(solution)/shard_map/all_gather | solution.py:85
  65.0 42.2 %copy-start.4 = (f32[8192]{0:T(1024)S(1)}, f32[8192]{0:T(1024)}, u32[]{:S(2)}) copy-start(f32[8192]{0:T(1024)} %param.21) | copy-start | bytes 98308
  104.9 2.3 %copy-start.1 = (bf16[128,8192]{1,0:T(8,128)(2,1)S(1)}, bf16[128,8192]{1,0:T(8,128)(2,1)}, u32[]{:S(2)}) copy-start(bf16[128,8192]{1,0:T(8,128)(2,1)} %all-gather.5.cloned.1.call-done) | copy-start | bytes 6291460
Sparse Core Ops, SparseCore 0:
  14.8 44.1 all-gather.2
  65.1 39.7 all-gather.4
where the time goes:
time: 132 us; the launch traced here: 131 us
  waiting for transfers between devices  84.2 us (64%)
  matrix products  25.7 us (19%)
  between operations  14.2 us (11%)
  other arithmetic  5 us (4%)
  local copies, waits for them, and re-layouts  2.08 us (2%)
    all_gather x1, waiting for transfers between devices, per_device(): gathered = lax.all_gather(attention, 'wide', axis=0, tiled=True)  44.3 us
    all_gather x1, waiting for transfers between devices, per_device(): whole = lax.all_gather(residual, 'wide', axis=1, tiled=True)  39.9 us
    dot_general x1, matrix products, per_device(): up_part = jnp.dot(normed, up_weight, preferred_element_type=jnp.float32)  9.04 us
    dot_general x1, matrix products, per_device(): gate = jnp.dot(normed, gate_weight, preferred_element_type=jnp.float32)  8.26 us
    dot_general x1, matrix products, per_device(): jnp.einsum('gtj,gjc->tc', stacked, out_weight.reshape(group_count, width,...  5.94 us
  transfers between devices with their start and end apart: 2, of which 2 were waited for; matrix products, arithmetic and copies ran while one was open for 0% of the time, Pallas kernels for 0%

commit v1 on v0

v1 whole, which is shorter than its diff:
```python
import math

import jax
import jax.numpy as jnp
from jax import lax
from jax.experimental import pallas as pl
from jax.experimental.pallas import tpu as pltpu
from jax.sharding import PartitionSpec as P

VMEM = pl.BlockSpec(memory_space=pltpu.VMEM)


def layout(size):
    cores = 2 if size % 2 == 0 else 1
    rows = 2 if (size // cores) % 2 == 0 else 1
    return size // (cores * rows), rows, cores


def attend(first_pair, queries, cache_keys, cache_values, new_keys, new_values, lengths, segments):
    pairs, steps, width = queries.shape
    slots, head = cache_keys.shape[1:]
    heads = width // head
    beams = lengths.shape[0]
    scale = 1.0 / math.sqrt(head)

    def kernel(first, lens, segs, q_ref, k_ref, v_ref, nk_ref, nv_ref, o_ref):
        beam = lax.rem(first[0] + pl.program_id(0), beams)
        q = q_ref[0]
        q = jnp.concatenate([q[:, i * head : (i + 1) * head] for i in range(heads)], axis=0)
        contract = (((1,), (1,)), ((), ()))
        old = lax.dot_general(q, k_ref[0], contract, preferred_element_type=jnp.float32) * scale
        new = lax.dot_general(q, nk_ref[0], contract, preferred_element_type=jnp.float32) * scale
        slot = lax.broadcasted_iota(jnp.int32, old.shape, 1)
        old = jnp.where(slot < lens[beam], old, -jnp.inf)
        row = lax.broadcasted_iota(jnp.int32, (steps, steps), 0)
        col = lax.broadcasted_iota(jnp.int32, (steps, steps), 1)
        seg_row = jnp.zeros((steps, steps), jnp.int32)
        seg_col = jnp.zeros((steps, steps), jnp.int32)
        for j in range(steps):
            value = segs[beam, j]
            seg_row = jnp.where(row == j, value, seg_row)
            seg_col = jnp.where(col == j, value, seg_col)
        bias = jnp.where((seg_row == seg_col) & (col <= row), 0.0, -jnp.inf)
        new = new + jnp.concatenate([bias] * heads, axis=0)
        top = jnp.maximum(
            jnp.max(old, axis=1, keepdims=True), jnp.max(new, axis=1, keepdims=True)
        )
        old = jnp.exp(old - top)
        new = jnp.exp(new - top)
        denom = jnp.sum(old, axis=1, keepdims=True) + jnp.sum(new, axis=1, keepdims=True)
        inverse = 1.0 / denom
        mixed = jnp.dot(
            (old * inverse).astype(jnp.bfloat16), v_ref[0], preferred_element_type=jnp.float32
        ) + jnp.dot(
            (new * inverse).astype(jnp.bfloat16), nv_ref[0], preferred_element_type=jnp.float32
        )
        mixed = mixed.astype(jnp.bfloat16)
        for i in range(heads):
            o_ref[:, i * head : (i + 1) * head] = mixed[i * steps : (i + 1) * steps]

    def whole(*shape):
        return pl.BlockSpec((1, *shape), lambda p, *_: (p, 0, 0))

    return pl.pallas_call(
        kernel,
        grid_spec=pltpu.PrefetchScalarGridSpec(
            num_scalar_prefetch=3,
            grid=(pairs,),
            in_specs=[
                whole(steps, width),
                whole(slots, head),
                whole(slots, head),
                whole(steps, head),
                whole(steps, head),
            ],
            out_specs=pl.BlockSpec((steps, width), lambda p, *_: (p, 0)),
        ),
        out_shape=jax.ShapeDtypeStruct((pairs * steps, width), jnp.bfloat16),
        compiler_params=pltpu.CompilerParams(vmem_limit_bytes=16 << 20),
        cost_estimate=pl.CostEstimate(
            flops=4 * pairs * steps * heads * slots * head,
            bytes_accessed=4 * pairs * slots * head,
            transcendentals=pairs * steps * heads * slots,
        ),
        name="attend",
    )(first_pair, lengths, segments, queries, cache_keys, cache_values, new_keys, new_values)


def spread(x, size):
    planes, rows, cores = layout(size)
    line = rows * cores
    assert cores == 2 and rows == 2

    def send(value, target):
        return lax.ppermute(value, "wide", [(i, target(i)) for i in range(size)])

    def shift(value, k):
        return send(value, lambda i: (i + k * line) % size)

    def cross(value):
        return send(value, lambda i: i ^ cores)

    def both(value):
        return value, send(value, lambda i: i ^ 1)

    def after(value, *others):
        return lax.optimization_barrier((value, *others))[0]

    rounds = [[both(x)]]
    near = sorted({1, planes - 1}) if planes > 1 else []
    far = [k for k in range(2, planes - 1)]
    got = [(k, shift(x, k)) for k in near]
    rounds.append([both(cross(x))])
    start = after(x, *[v for _, v in got])
    later = [(k, shift(start, k)) for k in far]
    for group in (got, later):
        if group:
            rounds.append([both(v) for _, v in group])
            rounds.append([both(cross(v)) for _, v in group])
    order = [(0, 0), (0, 1)]
    for group in (near, far):
        order += [(k, 0) for k in group] + [(k, 1) for k in group]
    return rounds, order


def project(table, base, first, last, acc, blocks, resid, weight, width, tokens):
    cols = weight.shape[1]
    half = blocks[0][0].shape[0]
    count = len(blocks)

    def kernel(tab, *refs):
        refs = list(refs)
        xs = [(refs.pop(0), refs.pop(0)) for _ in range(count)]
        w_ref = refs.pop(0)
        acc_ref = None if first else refs.pop(0)
        resid_ref = refs.pop(0) if last else None
        o_ref, joined, *rest = refs
        total = rest[0] if last else o_ref
        step = pl.program_id(0)

        @pl.when(step == 0)
        def _():
            total[...] = jnp.zeros_like(total) if first else acc_ref[...]

        own = tab[0, 0]
        for i in range(count):

            @pl.when(step == i)
            def _(i=i):
                joined[pl.ds(pl.multiple_of(own * half, half), half)] = xs[i][0][...]
                joined[pl.ds(pl.multiple_of((1 - own) * half, half), half)] = xs[i][1][...]

        at = pl.ds(pl.multiple_of(tab[2, base + step] * (2 * half), 2 * half), 2 * half)
        total[at] += jnp.dot(joined[...], w_ref[...], preferred_element_type=jnp.float32)
        if last:

            @pl.when(step == count - 1)
            def _():
                o_ref[...] = (resid_ref[...].astype(jnp.float32) + total[...]).astype(
                    jnp.bfloat16
                )

    inputs = [v for pair in blocks for v in pair] + [weight]
    specs = [pl.BlockSpec((half, width), lambda j, t: (0, 0))] * (2 * count) + [
        pl.BlockSpec((width, cols), lambda j, t: (t[1, base + j], 0))
    ]
    full = pl.BlockSpec((tokens, cols), lambda j, t: (0, 0))
    if not first:
        inputs.append(acc)
        specs.append(full)
    if last:
        inputs.append(resid)
        specs.append(full)
    scratch = [pltpu.VMEM((2 * half, width), jnp.bfloat16)]
    if last:
        scratch.append(pltpu.VMEM((tokens, cols), jnp.float32))
    return pl.pallas_call(
        kernel,
        grid_spec=pltpu.PrefetchScalarGridSpec(
            num_scalar_prefetch=1,
            grid=(count,),
            in_specs=specs,
            out_specs=full,
            scratch_shapes=scratch,
        ),
        out_shape=jax.ShapeDtypeStruct((tokens, cols), jnp.bfloat16 if last else jnp.float32),
        compiler_params=pltpu.CompilerParams(vmem_limit_bytes=16 << 20),
        cost_estimate=pl.CostEstimate(
            flops=4 * count * half * width * cols,
            bytes_accessed=2 * count * width * cols,
            transcendentals=0,
        ),
        name="project",
    )(table, *inputs)


def expand(table, base, first, last, state, blocks, gain, gate_weight, up_weight):
    flat = [v for pair in blocks for v in pair]
    count = len(flat)
    tokens, depth = flat[0].shape
    cols = gate_weight.shape[1]
    features = gate_weight.shape[0]
    lanes = 128

    def kernel(tab, *refs):
        refs = list(refs)
        xs = [refs.pop(0) for _ in range(count)]
        gain_ref, g_ref, u_ref = refs.pop(0), refs.pop(0), refs.pop(0)
        olds = [] if first else [refs.pop(0) for _ in range(3)]
        o_ref = refs.pop(0) if last else None
        gate, up, square = refs
        step = pl.program_id(0)

        @pl.when(step == 0)
        def _():
            for i, total in enumerate((gate, up, square)):
                total[...] = jnp.zeros_like(total) if first else olds[i][...]

        def add(x_ref):
            wide = x_ref[...].astype(jnp.float32)
            squares = wide * wide
            part = squares[:, :lanes]
            for i in range(1, depth // lanes):
                part = part + squares[:, i * lanes : (i + 1) * lanes]
            square[...] += part
            scaled = (wide * gain_ref[0]).astype(jnp.bfloat16)
            gate[...] += jnp.dot(scaled, g_ref[...], preferred_element_type=jnp.float32)
            up[...] += jnp.dot(scaled, u_ref[...], preferred_element_type=jnp.float32)

        for i in range(count):
            pl.when(step == i)(lambda i=i: add(xs[i]))
        if last:

            @pl.when(step == count - 1)
            def _():
                mean = jnp.sum(square[...], axis=1, keepdims=True) / features
                inverse = lax.rsqrt(mean + 1e-06)
                v = gate[...] * inverse
                o_ref[...] = (v / (1.0 + jnp.exp(-v)) * (up[...] * inverse)).astype(jnp.bfloat16)

    def row(j, t):
        return (t[3, base + j], 0)

    sums = [(tokens, cols), (tokens, cols), (tokens, lanes)]
    specs = [pl.BlockSpec((tokens, depth), lambda j, t: (0, 0))] * count + [
        pl.BlockSpec((1, 1, depth), lambda j, t: (t[3, base + j], 0, 0)),
        pl.BlockSpec((depth, cols), row),
        pl.BlockSpec((depth, cols), row),
    ]
    sum_specs = [pl.BlockSpec(s, lambda j, t: (0, 0)) for s in sums]
    sum_shapes = [jax.ShapeDtypeStruct(s, jnp.float32) for s in sums]
    if not first:
        specs += sum_specs
    return pl.pallas_call(
        kernel,
        grid_spec=pltpu.PrefetchScalarGridSpec(
            num_scalar_prefetch=1,
            grid=(count,),
            in_specs=specs,
            out_specs=sum_specs[0] if last else sum_specs,
            scratch_shapes=[pltpu.VMEM(s, jnp.float32) for s in sums] if last else [],
        ),
        out_shape=jax.ShapeDtypeStruct((tokens, cols), jnp.bfloat16) if last else sum_shapes,
        compiler_params=pltpu.CompilerParams(vmem_limit_bytes=24 << 20),
        cost_estimate=pl.CostEstimate(
            flops=4 * count * tokens * depth * cols,
            bytes_accessed=4 * count * depth * cols,
            transcendentals=0,
        ),
        name="expand",
    )(table, *flat, gain, gate_weight, up_weight, *([] if first else state))


def make(size):
    planes, rows, cores = layout(size)

    def per_device(
        queries,
        cache_keys,
        cache_values,
        new_keys,
        new_values,
        cache_lengths,
        step_segments,
        resid_in,
        out_weight,
        norm_gain,
        gate_weight,
        up_weight,
    ):
        pairs, steps, width = queries.shape
        beams = cache_lengths.shape[0]
        tokens, depth = resid_in.shape
        assert beams % (cores * pairs) == 0
        me = lax.axis_index("wide")
        attention = attend(
            jnp.full((1,), me * pairs, jnp.int32),
            queries,
            cache_keys,
            cache_values,
            new_keys,
            new_values,
            cache_lengths,
            step_segments,
        )
        rounds, order = spread(attention, size)
        plane, row, core = me // (rows * cores), me // cores % rows, me % cores
        shifts = jnp.array([k for k, _ in order], jnp.int32)
        flips = jnp.array([f for _, f in order], jnp.int32)
        chip = (plane - shifts + planes) % planes * rows + row * (1 - flips) + (1 - row) * flips
        pair_at = chip * (cores * pairs)
        head_at = pair_at // beams
        token_at = pair_at % beams // (cores * pairs)
        chips = len(order)
        devices = chip[:, None] * cores + jnp.array([0, 1], jnp.int32)[None, :] * (1 - 2 * core) + core
        table = jnp.zeros((4, chips * cores), jnp.int32)
        table = table.at[0, 0].set(core).at[1, :chips].set(head_at).at[2, :chips].set(token_at)
        table = table.at[3].set(devices.reshape(-1))
        acc, base = None, 0
        for i, blocks in enumerate(rounds):
            acc = project(
                table,
                base,
                i == 0,
                i == len(rounds) - 1,
                acc,
                blocks,
                resid_in,
                out_weight,
                width,
                tokens,
            )
            base += len(blocks)
        residual = acc
        rounds, _ = spread(residual, size)
        gain = norm_gain.reshape(size, 1, depth)
        state, base = None, 0
        for i, blocks in enumerate(rounds):
            state = expand(
                table,
                base,
                i == 0,
                i == len(rounds) - 1,
                state,
                blocks,
                gain,
                gate_weight,
                up_weight,
            )
            base += cores * len(blocks)
        return residual, state

    return per_device


def solution(mesh):
    placed = (
        P(("groups", "wide"), None, None),
        P(("groups", "wide"), None, None),
        P(("groups", "wide"), None, None),
        P(("groups", "wide"), None, None),
        P(("groups", "wide"), None, None),
        P("groups"),
        P("groups", None),
        P("groups", "wide"),
        P(None, "wide"),
        P(),
        P(None, "wide"),
        P(None, "wide"),
    )
    return jax.shard_map(
        make(mesh.shape["wide"]),
        mesh=mesh,
        in_specs=placed,
        out_specs=(P("groups", "wide"), P("groups", "wide")),
        check_vma=False,
    )
```

time: 132 us -> 90.3 us (0.68)
  waiting for transfers between devices: 84.2 us -> 20.1 us
  Pallas kernels: 0 us -> 31.3 us
  matrix products: 25.7 us -> 0 us
  starting transfers between devices: 0.08 us -> 22.2 us
  between operations: 14.2 us -> 1 us
  local copies, waits for them, and re-layouts: 2.08 us -> 14.3 us
  other arithmetic: 5 us -> 0.8 us
    all_gather x2 -> x0, waiting for transfers between devices: 84.2 us -> none  [the longest x1 44.3 us: per_device(): gathered = lax.all_gather(attention, 'wide', axis=0, tiled=True)]
    pallas_call x0 -> x13, Pallas kernels: none -> 31.3 us  [the longest x6 21.1 us: expand(): pl.pallas_call(kernel, grid_spec=pltpu.PrefetchScalarGridSpec(num_scalar_...]
    dot_general x7 -> x0, matrix products: 25.7 us -> none  [the longest x1 9.04 us: per_device(): up_part = jnp.dot(normed, up_weight, preferred_element_type=jnp.float32)]
    ppermute x0 -> x30, starting transfers between devices: none -> 22.2 us  [send(): return lax.ppermute(value, 'wide', [(i, target(i)) for i in range(size)])]
    ppermute x0 -> x30, waiting for transfers between devices: none -> 20.1 us  [send(): return lax.ppermute(value, 'wide', [(i, target(i)) for i in range(size)])]
    unnamed x13 -> x32, local copies, waits for them, and re-layouts: 1.37 us -> 13.8 us
    reduce_sum x5 -> x0, other arithmetic: 4.73 us -> none  [the longest x1 2.23 us: per_device(): inverse = lax.rsqrt(jnp.sum(wide_rows * wide_rows, axis=1) / D + 1e-06)]
  transfers between devices with their start and end apart: 2 -> 30, of which waited for: 2 -> 8; matrix products, arithmetic and copies ran while one was open for 0% -> 1% of each run, Pallas kernels for 0% -> 25%
where the time goes in v1:
time: 90.3 us; the launch traced here: 89.6 us
  Pallas kernels  31.3 us (35%)
  starting transfers between devices  22.2 us (25%)
  waiting for transfers between devices  20.1 us (22%)
  local copies, waits for them, and re-layouts  14.3 us (16%)
  between operations  1 us (1%)
    ppermute x30, starting transfers between devices, send(): return lax.ppermute(value, 'wide', [(i, target(i)) for i in range(size)])  22.2 us
    pallas_call x6, Pallas kernels, expand(): pl.pallas_call(kernel, grid_spec=pltpu.PrefetchScalarGridSpec(num_scalar_...  21.1 us
    ppermute x30, waiting for transfers between devices, send(): return lax.ppermute(value, 'wide', [(i, target(i)) for i in range(size)])  20.1 us
    unnamed x32, local copies, waits for them, and re-layouts  13.8 us
    pallas_call x6, Pallas kernels, project(): pl.pallas_call(kernel, grid_spec=pltpu.PrefetchScalarGridSpec(num_scalar_...  6.83 us
    pallas_call x1, Pallas kernels, attend(): pl.pallas_call(kernel, grid_spec=pltpu.PrefetchScalarGridSpec(num_scalar_...  3.33 us
  transfers between devices with their start and end apart: 30, of which 8 were waited for; matrix products, arithmetic and copies ran while one was open for 1% of the time, Pallas kernels for 25%

profile of v1, /device:TPU:0, one launch (start us, length us, event | category | flops | bytes accessed | tf_op | source)
XLA Modules:
  0.0 89.6 jit_solution(18163886618501476805)
XLA Ops:
  0.6 1.2 %copy-done.3 = bf16[4,1024,128]{2,1,0:T(8,128)(2,1)S(1)} copy-done((bf16[4,1024,128]{2,1,0:T(8,128)(2,1)S(1)}, bf16[4,1024,128]{2,1,0:T(8,128)(2,1)}, u32[]{:S(2)}) %copy-start.3) | copy-done | bytes 1048600
  1.9 1.2 %copy-done.4 = bf16[4,1024,128]{2,1,0:T(8,128)(2,1)S(1)} copy-done((bf16[4,1024,128]{2,1,0:T(8,128)(2,1)S(1)}, bf16[4,1024,128]{2,1,0:T(8,128)(2,1)}, u32[]{:S(2)}) %copy-start.4) | copy-done | bytes 1048600
  3.1 0.9 %copy-done.7 = bf16[4,16,1024]{2,1,0:T(8,128)(2,1)S(1)} copy-done((bf16[4,16,1024]{2,1,0:T(8,128)(2,1)S(1)}, bf16[4,16,1024]{2,1,0:T(8,128)(2,1)}, u32[]{:S(2)}) %copy-start.7) | copy-done | bytes 131096
  4.0 0.7 copy-done.8
  4.7 0.7 copy-done.9
  5.4 0.7 copy-done.10
  6.1 0.7 copy-done.11
  6.8 3.3 %attend.1.refs_0_ = bf16[64,1024]{1,0:T(8,128)(2,1)S(1)} custom-call(s32[1]{0:T(128)} %bitcast.3.first, s32[8]{0:T(128)S(1)} %copy-done.11, s32[8,16]{1,0:T(8,128)S(1)} %copy-done.10, bf16[4,16,1024]{2,1,0:T(8,128)(2,1)S(1)} %copy-done.7, bf16[4,1024,128]{2,1,0:T(8,128)(2,1)S(1)} %copy-done.3, bf16[4,1024,128]{2,1,0:T(8,128)(2,1)S(1)} %copy-done.4, ...), custom_call_target="tpu_custom_call" | custom-call | flops 268435456 | bytes 2097152 | tf_op jit(solution)/shard_map/attend/pallas_call | solution.py:64
  10.1 0.6 collective-permute-start.14
  10.7 2.6 %collective-permute-start.12 = (bf16[64,1024]{1,0:T(8,128)(2,1)S(1)}, bf16[64,1024]{1,0:T(8,128)(2,1)S(1)}, u32[]{:S(2)}, u32[]{:S(2)}) collective-permute-start(bf16[64,1024]{1,0:T(8,128)(2,1)S(1)} %attend.1.refs_0_), channel_id=1, source_target_pairs={{0,2},{1,3},{2,0},{3,1},{4,6},{5,7},{6,4},{7,5},{8,10},{9,11},{10,... | collective-permute-start | bytes 393224 | tf_op jit(solution)/shard_map/ppermute | solution.py:95
  13.2 1.6 %collective-permute-start = (bf16[64,1024]{1,0:T(8,128)(2,1)S(1)}, bf16[64,1024]{1,0:T(8,128)(2,1)S(1)}, u32[]{:S(2)}, u32[]{:S(2)}) collective-permute-start(bf16[64,1024]{1,0:T(8,128)(2,1)S(1)} %attend.1.refs_0_), channel_id=1, source_target_pairs={{0,4},{1,5},{2,6},{3,7},{4,8},{5,9},{6,10},{7,11},{8,12},{9,13},{1... | collective-permute-start | bytes 393224 | tf_op jit(solution)/shard_map/ppermute | solution.py:95
  14.8 2.2 %collective-permute-start.1 = (bf16[64,1024]{1,0:T(8,128)(2,1)S(1)}, bf16[64,1024]{1,0:T(8,128)(2,1)S(1)}, u32[]{:S(2)}, u32[]{:S(2)}) collective-permute-start(bf16[64,1024]{1,0:T(8,128)(2,1)S(1)} %attend.1.refs_0_), channel_id=1, source_target_pairs={{0,12},{1,13},{2,14},{3,15},{4,0},{5,1},{6,2},{7,3},{8,4},{9,5},{1... | collective-permute-start | bytes 393224 | tf_op jit(solution)/shard_map/ppermute | solution.py:95
  17.1 0.7 broadcast_multiply_fusion.1
  17.8 3.6 %collective-permute-done.refs_0_ = bf16[64,1024]{1,0:T(8,128)(2,1)S(1)} collective-permute-done((bf16[64,1024]{1,0:T(8,128)(2,1)S(1)}, bf16[64,1024]{1,0:T(8,128)(2,1)S(1)}, u32[]{:S(2)}, u32[]{:S(2)}) %collective-permute-start) | collective-permute-done | bytes 131104 | tf_op jit(solution)/shard_map/ppermute | solution.py:95
  21.4 1.5 %collective-permute-done.1.refs_2_ = bf16[64,1024]{1,0:T(8,128)(2,1)S(1)} collective-permute-done((bf16[64,1024]{1,0:T(8,128)(2,1)S(1)}, bf16[64,1024]{1,0:T(8,128)(2,1)S(1)}, u32[]{:S(2)}, u32[]{:S(2)}) %collective-permute-start.1) | collective-permute-done | bytes 131104 | tf_op jit(solution)/shard_map/ppermute | solution.py:95
  22.9 1.3 %collective-permute-start.2 = (bf16[64,1024]{1,0:T(8,128)(2,1)S(1)}, bf16[64,1024]{1,0:T(8,128)(2,1)S(1)}, u32[]{:S(2)}, u32[]{:S(2)}) collective-permute-start(bf16[64,1024]{1,0:T(8,128)(2,1)S(1)} %attend.1.refs_0_), channel_id=1, source_target_pairs={{0,8},{1,9},{2,10},{3,11},{4,12},{5,13},{6,14},{7,15},{8,0},{9,1},... | collective-permute-start | bytes 393224 | tf_op jit(solution)/shard_map/ppermute | solution.py:95
  24.2 0.1 add_add_fusion
  24.3 0.5 collective-permute-start.6
  24.8 1.5 %collective-permute-start.8 = (bf16[64,1024]{1,0:T(8,128)(2,1)S(1)}, bf16[64,1024]{1,0:T(8,128)(2,1)S(1)}, u32[]{:S(2)}, u32[]{:S(2)}) collective-permute-start(bf16[64,1024]{1,0:T(8,128)(2,1)S(1)} %collective-permute-done.1.refs_2_), channel_id=1, source_target_pairs={{0,2},{1,3},{2,0},{3,1},{4,6},{5,7},{6,4},{7,5},{8,10},{9,11},{10,... | collective-permute-start | bytes 393224 | tf_op jit(solution)/shard_map/ppermute | solution.py:95
  26.3 5.2 %collective-permute-done.2.refs_0_ = bf16[64,1024]{1,0:T(8,128)(2,1)S(1)} collective-permute-done((bf16[64,1024]{1,0:T(8,128)(2,1)S(1)}, bf16[64,1024]{1,0:T(8,128)(2,1)S(1)}, u32[]{:S(2)}, u32[]{:S(2)}) %collective-permute-start.2) | collective-permute-done | bytes 131104 | tf_op jit(solution)/shard_map/ppermute | solution.py:95
  31.5 0.5 collective-permute-start.3
  32.0 0.1 collective-permute-start.11
  32.1 0.5 collective-permute-start.5
  32.6 0.1 collective-permute-start.7
  32.7 0.4 collective-permute-done.8.refs_2_
  33.0 0.1 collective-permute-start.9
  33.1 3.3 %collective-permute-done.3.refs_0_ = bf16[64,1024]{1,0:T(8,128)(2,1)S(1)} collective-permute-done((bf16[64,1024]{1,0:T(8,128)(2,1)S(1)}, bf16[64,1024]{1,0:T(8,128)(2,1)S(1)}, u32[]{:S(2)}, u32[]{:S(2)}) %collective-permute-start.3) | collective-permute-done | bytes 131104 | tf_op jit(solution)/shard_map/ppermute | solution.py:95
  36.5 0.1 add.89
  36.5 0.2 scatter.15
  36.7 0.2 scatter.16
  36.9 3.4 %copy-done = bf16[8192,512]{1,0:T(8,128)(2,1)S(1)} copy-done((bf16[8192,512]{1,0:T(8,128)(2,1)S(1)}, bf16[8192,512]{1,0:T(8,128)(2,1)}, u32[]{:S(2)}) %copy-start) | copy-done | bytes 8388632
  40.3 0.9 project.6.refs_3_
  41.2 3.4 %copy-done.1 = bf16[8192,512]{1,0:T(8,128)(2,1)S(1)} copy-done((bf16[8192,512]{1,0:T(8,128)(2,1)S(1)}, bf16[8192,512]{1,0:T(8,128)(2,1)}, u32[]{:S(2)}) %copy-start.1) | copy-done | bytes 8388632
  44.6 0.9 project.7.refs_5_
  45.5 0.0 slice-start
  45.5 0.0 copy-start.2
  45.5 1.3 %project.8.refs_5_ = f32[128,512]{1,0:T(8,128)S(1)} custom-call(s32[4,16]{1,0:T(4,128)S(1)} %scatter.19.tab, bf16[64,1024]{1,0:T(8,128)(2,1)S(1)} %collective-permute-done.refs_0_, bf16[64,1024]{1,0:T(8,128)(2,1)S(1)} %collective-permute-done.10.refs_1_, bf16[64,1024]{1,0:T(8,128)(2,1)S(1)} %collective-permute-done.1.refs_2_, ...), custom_call_target="tpu_custom_call" | custom-call | flops 268435456 | bytes 2097152 | tf_op jit(solution)/shard_map/project/pallas_call | solution.py:177
  46.8 0.0 slice-start.2
  46.9 1.3 %project.9.refs_3_ = f32[128,512]{1,0:T(8,128)S(1)} custom-call(s32[4,16]{1,0:T(4,128)S(1)} %scatter.19.tab, bf16[64,1024]{1,0:T(8,128)(2,1)S(1)} %collective-permute-done.6.refs_0_, bf16[64,1024]{1,0:T(8,128)(2,1)S(1)} %collective-permute-done.7.refs_1_, bf16[64,1024]{1,0:T(8,128)(2,1)S(1)} %collective-permute-done.8.refs_2_, ...), custom_call_target="tpu_custom_call" | custom-call | flops 268435456 | bytes 2097152 | tf_op jit(solution)/shard_map/project/pallas_call | solution.py:177
  48.2 0.0 slice-start.3
  48.2 0.9 project.10.refs_3_
  49.1 1.6 %project.11.refs_0_ = bf16[128,512]{1,0:T(8,128)(2,1)} custom-call(s32[4,16]{1,0:T(4,128)S(1)} %scatter.19.tab, bf16[64,1024]{1,0:T(8,128)(2,1)S(1)} %collective-permute-done.3.refs_0_, bf16[64,1024]{1,0:T(8,128)(2,1)S(1)} %collective-permute-done.4.refs_1_, bf16[8192,512]{1,0:T(8,128)(2,1)S(1)} %copy-done.1, f32[128,512]{1,0:T(8,128)S(1)} %project.10.refs_3_, ...), custom_call_target="tpu_custom_call" | custom-call | flops 134217728 | bytes 1048576 | tf_op jit(solution)/shard_map/project/pallas_call | solution.py:177
  50.7 0.5 collective-permute-start.27
  51.2 0.9 %collective-permute-start.15 = (bf16[128,512]{1,0:T(8,128)(2,1)}, bf16[128,512]{1,0:T(8,128)(2,1)S(1)}, u32[]{:S(2)}, u32[]{:S(2)}) collective-permute-start(bf16[128,512]{1,0:T(8,128)(2,1)} %project.11.refs_0_), channel_id=1, source_target_pairs={{0,4},{1,5},{2,6},{3,7},{4,8},{5,9},{6,10},{7,11},{8,12},{9,13},{1... | collective-permute-start | bytes 393224 | tf_op jit(solution)/shard_map/ppermute | solution.py:95
  52.1 2.9 %collective-permute-start.16 = (bf16[128,512]{1,0:T(8,128)(2,1)}, bf16[128,512]{1,0:T(8,128)(2,1)S(1)}, u32[]{:S(2)}, u32[]{:S(2)}) collective-permute-start(bf16[128,512]{1,0:T(8,128)(2,1)} %project.11.refs_0_), channel_id=1, source_target_pairs={{0,12},{1,13},{2,14},{3,15},{4,0},{5,1},{6,2},{7,3},{8,4},{9,5},{1... | collective-permute-start | bytes 393224 | tf_op jit(solution)/shard_map/ppermute | solution.py:95
  55.0 1.8 %collective-permute-done.27.refs_0_ = bf16[128,512]{1,0:T(8,128)(2,1)S(1)} collective-permute-done((bf16[128,512]{1,0:T(8,128)(2,1)}, bf16[128,512]{1,0:T(8,128)(2,1)S(1)}, u32[]{:S(2)}, u32[]{:S(2)}) %collective-permute-start.27) | collective-permute-done | bytes 131104 | tf_op jit(solution)/shard_map/ppermute | solution.py:95
  56.8 2.8 %collective-permute-done.15.refs_0_ = bf16[128,512]{1,0:T(8,128)(2,1)S(1)} collective-permute-done((bf16[128,512]{1,0:T(8,128)(2,1)}, bf16[128,512]{1,0:T(8,128)(2,1)S(1)}, u32[]{:S(2)}, u32[]{:S(2)}) %collective-permute-start.15) | collective-permute-done | bytes 131104 | tf_op jit(solution)/shard_map/ppermute | solution.py:95
  59.6 1.5 %collective-permute-start.21 = (bf16[128,512]{1,0:T(8,128)(2,1)S(1)}, bf16[128,512]{1,0:T(8,128)(2,1)S(1)}, u32[]{:S(2)}, u32[]{:S(2)}) collective-permute-start(bf16[128,512]{1,0:T(8,128)(2,1)S(1)} %collective-permute-done.15.refs_0_), channel_id=1, source_target_pairs={{0,2},{1,3},{2,0},{3,1},{4,6},{5,7},{6,4},{7,5},{8,10},{9,11},{10,... | collective-permute-start | bytes 393224 | tf_op jit(solution)/shard_map/ppermute | solution.py:95
  61.1 0.9 collective-permute-start.23
  62.0 1.7 %collective-permute-start.17 = (bf16[128,512]{1,0:T(8,128)(2,1)}, bf16[128,512]{1,0:T(8,128)(2,1)S(1)}, u32[]{:S(2)}, u32[]{:S(2)}) collective-permute-start(bf16[128,512]{1,0:T(8,128)(2,1)} %project.11.refs_0_), channel_id=1, source_target_pairs={{0,8},{1,9},{2,10},{3,11},{4,12},{5,13},{6,14},{7,15},{8,0},{9,1},... | collective-permute-start | bytes 393224 | tf_op jit(solution)/shard_map/ppermute | solution.py:95
  63.8 0.5 collective-permute-start.26
  64.3 0.9 copy-done.5
  65.2 2.8 %expand.6 = (f32[128,1024]{1,0:T(8,128)S(1)}, f32[128,1024]{1,0:T(8,128)S(1)}, f32[128,128]{1,0:T(8,128)S(1)}) custom-call(s32[4,16]{1,0:T(4,128)S(1)} %scatter.19.tab, bf16[128,512]{1,0:T(8,128)(2,1)S(1)} %copy-done.5, bf16[128,512]{1,0:T(8,128)(2,1)S(1)} %collective-permute-done.29.refs_1_, f32[16,1,512]{2,1,0:T(1,128)S(1)} %bitcast.9, ...), custom_call_target="tpu_custom_call" | custom-call | flops 536870912 | bytes 4194304 | tf_op jit(solution)/shard_map/expand/pallas_call | solution.py:254
  68.0 0.1 collective-permute-start.22
  68.1 0.4 collective-permute-start.24
  68.6 1.4 %collective-permute-done.17.refs_0_ = bf16[128,512]{1,0:T(8,128)(2,1)S(1)} collective-permute-done((bf16[128,512]{1,0:T(8,128)(2,1)}, bf16[128,512]{1,0:T(8,128)(2,1)S(1)}, u32[]{:S(2)}, u32[]{:S(2)}) %collective-permute-start.17) | collective-permute-done | bytes 131104 | tf_op jit(solution)/shard_map/ppermute | solution.py:95
  70.0 0.5 collective-permute-start.18
  70.5 2.8 %expand.7 = (f32[128,1024]{1,0:T(8,128)S(1)}, f32[128,1024]{1,0:T(8,128)S(1)}, f32[128,128]{1,0:T(8,128)S(1)}) custom-call(s32[4,16]{1,0:T(4,128)S(1)} %scatter.19.tab, bf16[128,512]{1,0:T(8,128)(2,1)S(1)} %collective-permute-done.27.refs_0_, bf16[128,512]{1,0:T(8,128)(2,1)S(1)} %collective-permute-done.28.refs_1_, f32[16,1,512]{2,1,0:T(1,128)S(1)} %bitcast.10, ...), custom_call_target="tpu_custom_call" | custom-call | flops 536870912 | bytes 4194304 | tf_op jit(solution)/shard_map/expand/pallas_call | solution.py:254
  73.4 0.1 collective-permute-start.20
  73.4 4.6 %expand.8 = (f32[128,1024]{1,0:T(8,128)S(1)}, f32[128,1024]{1,0:T(8,128)S(1)}, f32[128,128]{1,0:T(8,128)S(1)}) custom-call(s32[4,16]{1,0:T(4,128)S(1)} %scatter.19.tab, bf16[128,512]{1,0:T(8,128)(2,1)S(1)} %collective-permute-done.15.refs_0_, bf16[128,512]{1,0:T(8,128)(2,1)S(1)} %collective-permute-done.25.refs_1_, ...), custom_call_target="tpu_custom_call" | custom-call | flops 1073741824 | bytes 8388608 | tf_op jit(solution)/shard_map/expand/pallas_call | solution.py:254
  78.1 0.5 collective-permute-start.19
  78.6 4.6 %expand.9 = (f32[128,1024]{1,0:T(8,128)S(1)}, f32[128,1024]{1,0:T(8,128)S(1)}, f32[128,128]{1,0:T(8,128)S(1)}) custom-call(s32[4,16]{1,0:T(4,128)S(1)} %scatter.19.tab, bf16[128,512]{1,0:T(8,128)(2,1)S(1)} %collective-permute-done.21.refs_0_, bf16[128,512]{1,0:T(8,128)(2,1)S(1)} %collective-permute-done.22.refs_1_, ...), custom_call_target="tpu_custom_call" | custom-call | flops 1073741824 | bytes 8388608 | tf_op jit(solution)/shard_map/expand/pallas_call | solution.py:254
  83.3 2.8 %expand.10 = (f32[128,1024]{1,0:T(8,128)S(1)}, f32[128,1024]{1,0:T(8,128)S(1)}, f32[128,128]{1,0:T(8,128)S(1)}) custom-call(s32[4,16]{1,0:T(4,128)S(1)} %scatter.19.tab, bf16[128,512]{1,0:T(8,128)(2,1)S(1)} %collective-permute-done.17.refs_0_, bf16[128,512]{1,0:T(8,128)(2,1)S(1)} %collective-permute-done.20.refs_1_, f32[16,1,512]{2,1,0:T(1,128)S(1)} %bitcast.13, ...), custom_call_target="tpu_custom_call" | custom-call | flops 536870912 | bytes 4194304 | tf_op jit(solution)/shard_map/expand/pallas_call | solution.py:254
  86.1 3.5 %expand.11 = bf16[128,1024]{1,0:T(8,128)(2,1)} custom-call(s32[4,16]{1,0:T(4,128)S(1)} %scatter.19.tab, bf16[128,512]{1,0:T(8,128)(2,1)S(1)} %collective-permute-done.18.refs_0_, bf16[128,512]{1,0:T(8,128)(2,1)S(1)} %collective-permute-done.19.refs_1_, f32[16,1,512]{2,1,0:T(1,128)S(1)} %bitcast.14, bf16[8192,1024]{1,0:T(8,128)(2,1)S(1)} %bitcast.8, ...), custom_call_target="tpu_custom_call" | custom-call | flops 536870912 | bytes 4194304 | tf_op jit(solution)/shard_map/expand/pallas_call | solution.py:254
  (52 shorter events, 0.2 us)
Async XLA Ops:
  0.6 1.2 %copy-start.3 = (bf16[4,1024,128]{2,1,0:T(8,128)(2,1)S(1)}, bf16[4,1024,128]{2,1,0:T(8,128)(2,1)}, u32[]{:S(2)}) copy-start(bf16[4,1024,128]{2,1,0:T(8,128)(2,1)} %k_ref.1) | copy-start | bytes 3145732
  1.9 1.2 %copy-start.4 = (bf16[4,1024,128]{2,1,0:T(8,128)(2,1)S(1)}, bf16[4,1024,128]{2,1,0:T(8,128)(2,1)}, u32[]{:S(2)}) copy-start(bf16[4,1024,128]{2,1,0:T(8,128)(2,1)} %v_ref.1) | copy-start | bytes 3145732
  3.1 0.9 %copy-start.7 = (bf16[4,16,1024]{2,1,0:T(8,128)(2,1)S(1)}, bf16[4,16,1024]{2,1,0:T(8,128)(2,1)}, u32[]{:S(2)}) copy-start(bf16[4,16,1024]{2,1,0:T(8,128)(2,1)} %q_ref.1) | copy-start | bytes 393220
  4.0 0.7 copy-start.8
  4.7 0.7 copy-start.9
  5.4 0.7 copy-start.10
  6.1 0.7 copy-start.11
  10.1 14.7 %collective-permute-start.14 = (bf16[64,1024]{1,0:T(8,128)(2,1)S(1)}, bf16[64,1024]{1,0:T(8,128)(2,1)S(1)}, u32[]{:S(2)}, u32[]{:S(2)}) collective-permute-start(bf16[64,1024]{1,0:T(8,128)(2,1)S(1)} %attend.1.refs_0_), channel_id=1, source_target_pairs={{0,1},{1,0},{2,3},{3,2},{4,5},{5,4},{6,7},{7,6},{8,9},{9,8},{10,11... | collective-permute-start | bytes 393224 | tf_op jit(solution)/shard_map/ppermute | solution.py:95
  10.7 15.6 %collective-permute-start.12 = (bf16[64,1024]{1,0:T(8,128)(2,1)S(1)}, bf16[64,1024]{1,0:T(8,128)(2,1)S(1)}, u32[]{:S(2)}, u32[]{:S(2)}) collective-permute-start(bf16[64,1024]{1,0:T(8,128)(2,1)S(1)} %attend.1.refs_0_), channel_id=1, source_target_pairs={{0,2},{1,3},{2,0},{3,1},{4,6},{5,7},{6,4},{7,5},{8,10},{9,11},{10,... | collective-permute-start | bytes 393224 | tf_op jit(solution)/shard_map/ppermute | solution.py:95
  13.2 8.2 %collective-permute-start = (bf16[64,1024]{1,0:T(8,128)(2,1)S(1)}, bf16[64,1024]{1,0:T(8,128)(2,1)S(1)}, u32[]{:S(2)}, u32[]{:S(2)}) collective-permute-start(bf16[64,1024]{1,0:T(8,128)(2,1)S(1)} %attend.1.refs_0_), channel_id=1, source_target_pairs={{0,4},{1,5},{2,6},{3,7},{4,8},{5,9},{6,10},{7,11},{8,12},{9,13},{1... | collective-permute-start | bytes 393224 | tf_op jit(solution)/shard_map/ppermute | solution.py:95
  14.8 8.1 %collective-permute-start.1 = (bf16[64,1024]{1,0:T(8,128)(2,1)S(1)}, bf16[64,1024]{1,0:T(8,128)(2,1)S(1)}, u32[]{:S(2)}, u32[]{:S(2)}) collective-permute-start(bf16[64,1024]{1,0:T(8,128)(2,1)S(1)} %attend.1.refs_0_), channel_id=1, source_target_pairs={{0,12},{1,13},{2,14},{3,15},{4,0},{5,1},{6,2},{7,3},{8,4},{9,5},{1... | collective-permute-start | bytes 393224 | tf_op jit(solution)/shard_map/ppermute | solution.py:95
  22.9 8.6 %collective-permute-start.2 = (bf16[64,1024]{1,0:T(8,128)(2,1)S(1)}, bf16[64,1024]{1,0:T(8,128)(2,1)S(1)}, u32[]{:S(2)}, u32[]{:S(2)}) collective-permute-start(bf16[64,1024]{1,0:T(8,128)(2,1)S(1)} %attend.1.refs_0_), channel_id=1, source_target_pairs={{0,8},{1,9},{2,10},{3,11},{4,12},{5,13},{6,14},{7,15},{8,0},{9,1},... | collective-permute-start | bytes 393224 | tf_op jit(solution)/shard_map/ppermute | solution.py:95
  24.3 7.8 %collective-permute-start.10 = (bf16[64,1024]{1,0:T(8,128)(2,1)S(1)}, bf16[64,1024]{1,0:T(8,128)(2,1)S(1)}, u32[]{:S(2)}, u32[]{:S(2)}) collective-permute-start(bf16[64,1024]{1,0:T(8,128)(2,1)S(1)} %collective-permute-done.refs_0_), channel_id=1, source_target_pairs={{0,1},{1,0},{2,3},{3,2},{4,5},{5,4},{6,7},{7,6},{8,9},{9,8},{10,11... | collective-permute-start | bytes 393224 | tf_op jit(solution)/shard_map/ppermute | solution.py:95
  24.3 8.3 %collective-permute-start.6 = (bf16[64,1024]{1,0:T(8,128)(2,1)S(1)}, bf16[64,1024]{1,0:T(8,128)(2,1)S(1)}, u32[]{:S(2)}, u32[]{:S(2)}) collective-permute-start(bf16[64,1024]{1,0:T(8,128)(2,1)S(1)} %collective-permute-done.refs_0_), channel_id=1, source_target_pairs={{0,2},{1,3},{2,0},{3,1},{4,6},{5,7},{6,4},{7,5},{8,10},{9,11},{10,... | collective-permute-start | bytes 393224 | tf_op jit(solution)/shard_map/ppermute | solution.py:95
  24.8 8.3 %collective-permute-start.8 = (bf16[64,1024]{1,0:T(8,128)(2,1)S(1)}, bf16[64,1024]{1,0:T(8,128)(2,1)S(1)}, u32[]{:S(2)}, u32[]{:S(2)}) collective-permute-start(bf16[64,1024]{1,0:T(8,128)(2,1)S(1)} %collective-permute-done.1.refs_2_), channel_id=1, source_target_pairs={{0,2},{1,3},{2,0},{3,1},{4,6},{5,7},{6,4},{7,5},{8,10},{9,11},{10,... | collective-permute-start | bytes 393224 | tf_op jit(solution)/shard_map/ppermute | solution.py:95
  26.3 5.7 %collective-permute-start.13 = (bf16[64,1024]{1,0:T(8,128)(2,1)S(1)}, bf16[64,1024]{1,0:T(8,128)(2,1)S(1)}, u32[]{:S(2)}, u32[]{:S(2)}) collective-permute-start(bf16[64,1024]{1,0:T(8,128)(2,1)S(1)} %collective-permute-done.12.refs_0_), channel_id=1, source_target_pairs={{0,1},{1,0},{2,3},{3,2},{4,5},{5,4},{6,7},{7,6},{8,9},{9,8},{10,11... | collective-permute-start | bytes 393224 | tf_op jit(solution)/shard_map/ppermute | solution.py:95
  31.5 5.0 %collective-permute-start.3 = (bf16[64,1024]{1,0:T(8,128)(2,1)S(1)}, bf16[64,1024]{1,0:T(8,128)(2,1)S(1)}, u32[]{:S(2)}, u32[]{:S(2)}) collective-permute-start(bf16[64,1024]{1,0:T(8,128)(2,1)S(1)} %collective-permute-done.2.refs_0_), channel_id=1, source_target_pairs={{0,2},{1,3},{2,0},{3,1},{4,6},{5,7},{6,4},{7,5},{8,10},{9,11},{10,... | collective-permute-start | bytes 393224 | tf_op jit(solution)/shard_map/ppermute | solution.py:95
  32.0 13.5 %collective-permute-start.11 = (bf16[64,1024]{1,0:T(8,128)(2,1)S(1)}, bf16[64,1024]{1,0:T(8,128)(2,1)S(1)}, u32[]{:S(2)}, u32[]{:S(2)}) collective-permute-start(bf16[64,1024]{1,0:T(8,128)(2,1)S(1)} %collective-permute-done.1.refs_2_), channel_id=1, source_target_pairs={{0,1},{1,0},{2,3},{3,2},{4,5},{5,4},{6,7},{7,6},{8,9},{9,8},{10,11... | collective-permute-start | bytes 393224 | tf_op jit(solution)/shard_map/ppermute | solution.py:95
  32.1 16.1 %collective-permute-start.5 = (bf16[64,1024]{1,0:T(8,128)(2,1)S(1)}, bf16[64,1024]{1,0:T(8,128)(2,1)S(1)}, u32[]{:S(2)}, u32[]{:S(2)}) collective-permute-start(bf16[64,1024]{1,0:T(8,128)(2,1)S(1)} %collective-permute-done.2.refs_0_), channel_id=1, source_target_pairs={{0,1},{1,0},{2,3},{3,2},{4,5},{5,4},{6,7},{7,6},{8,9},{9,8},{10,11... | collective-permute-start | bytes 393224 | tf_op jit(solution)/shard_map/ppermute | solution.py:95
  32.6 14.2 %collective-permute-start.7 = (bf16[64,1024]{1,0:T(8,128)(2,1)S(1)}, bf16[64,1024]{1,0:T(8,128)(2,1)S(1)}, u32[]{:S(2)}, u32[]{:S(2)}) collective-permute-start(bf16[64,1024]{1,0:T(8,128)(2,1)S(1)} %collective-permute-done.6.refs_0_), channel_id=1, source_target_pairs={{0,1},{1,0},{2,3},{3,2},{4,5},{5,4},{6,7},{7,6},{8,9},{9,8},{10,11... | collective-permute-start | bytes 393224 | tf_op jit(solution)/shard_map/ppermute | solution.py:95
  33.0 13.8 %collective-permute-start.9 = (bf16[64,1024]{1,0:T(8,128)(2,1)S(1)}, bf16[64,1024]{1,0:T(8,128)(2,1)S(1)}, u32[]{:S(2)}, u32[]{:S(2)}) collective-permute-start(bf16[64,1024]{1,0:T(8,128)(2,1)S(1)} %collective-permute-done.8.refs_2_), channel_id=1, source_target_pairs={{0,1},{1,0},{2,3},{3,2},{4,5},{5,4},{6,7},{7,6},{8,9},{9,8},{10,11... | collective-permute-start | bytes 393224 | tf_op jit(solution)/shard_map/ppermute | solution.py:95
  36.4 12.7 %collective-permute-start.4 = (bf16[64,1024]{1,0:T(8,128)(2,1)S(1)}, bf16[64,1024]{1,0:T(8,128)(2,1)S(1)}, u32[]{:S(2)}, u32[]{:S(2)}) collective-permute-start(bf16[64,1024]{1,0:T(8,128)(2,1)S(1)} %collective-permute-done.3.refs_0_), channel_id=1, source_target_pairs={{0,1},{1,0},{2,3},{3,2},{4,5},{5,4},{6,7},{7,6},{8,9},{9,8},{10,11... | collective-permute-start | bytes 393224 | tf_op jit(solution)/shard_map/ppermute | solution.py:95
  36.9 3.4 %copy-start = (bf16[8192,512]{1,0:T(8,128)(2,1)S(1)}, bf16[8192,512]{1,0:T(8,128)(2,1)}, u32[]{:S(2)}) copy-start(bf16[8192,512]{1,0:T(8,128)(2,1)} %refs_2_.7) | copy-start | bytes 25165828
  41.2 3.4 %copy-start.1 = (bf16[8192,512]{1,0:T(8,128)(2,1)S(1)}, bf16[8192,512]{1,0:T(8,128)(2,1)}, u32[]{:S(2)}) copy-start(bf16[8192,512]{1,0:T(8,128)(2,1)} %refs_2_.7) | copy-start | bytes 25165828
  44.6 4.5 %copy-start.6 = (bf16[128,512]{1,0:T(8,128)(2,1)S(1)}, bf16[128,512]{1,0:T(8,128)(2,1)}, u32[]{:S(2)}) copy-start(bf16[128,512]{1,0:T(8,128)(2,1)} %refs_4_.9) | copy-start | bytes 393220
  45.5 18.8 %slice-start = ((s8[16777216]{0:T(1024)(128)(4,1)}), s8[4194304]{0:T(1024)(128)(4,1)S(1)}, s32[]{:S(2)}) async-start(s8[16777216]{0:T(1024)(128)(4,1)} %bitcast.7), calls=%async_computation | async-start | bytes 8388608
  45.5 18.8 %slice-start.1 = ((s8[16777216]{0:T(1024)(128)(4,1)}), s8[4194304]{0:T(1024)(128)(4,1)S(1)}, s32[]{:S(2)}) async-start(s8[16777216]{0:T(1024)(128)(4,1)} %bitcast.7), calls=%async_computation.1 | async-start | bytes 8388608
  45.5 18.8 %copy-start.2 = (f32[8192]{0:T(1024)S(1)}, f32[8192]{0:T(1024)}, u32[]{:S(2)}) copy-start(f32[8192]{0:T(1024)} %param.32) | copy-start | bytes 98308
  46.8 17.5 %slice-start.2 = ((s8[16777216]{0:T(1024)(128)(4,1)}), s8[4194304]{0:T(1024)(128)(4,1)S(1)}, s32[]{:S(2)}) async-start(s8[16777216]{0:T(1024)(128)(4,1)} %bitcast.7), calls=%async_computation.2 | async-start | bytes 8388608
  48.2 16.1 %slice-start.3 = ((s8[16777216]{0:T(1024)(128)(4,1)}), s8[4194304]{0:T(1024)(128)(4,1)S(1)}, s32[]{:S(2)}) async-start(s8[16777216]{0:T(1024)(128)(4,1)} %bitcast.7), calls=%async_computation.3 | async-start | bytes 8388608
  50.7 6.1 %collective-permute-start.27 = (bf16[128,512]{1,0:T(8,128)(2,1)}, bf16[128,512]{1,0:T(8,128)(2,1)S(1)}, u32[]{:S(2)}, u32[]{:S(2)}) collective-permute-start(bf16[128,512]{1,0:T(8,128)(2,1)} %project.11.refs_0_), channel_id=1, source_target_pairs={{0,2},{1,3},{2,0},{3,1},{4,6},{5,7},{6,4},{7,5},{8,10},{9,11},{10,... | collective-permute-start | bytes 393224 | tf_op jit(solution)/shard_map/ppermute | solution.py:95
  51.2 8.4 %collective-permute-start.15 = (bf16[128,512]{1,0:T(8,128)(2,1)}, bf16[128,512]{1,0:T(8,128)(2,1)S(1)}, u32[]{:S(2)}, u32[]{:S(2)}) collective-permute-start(bf16[128,512]{1,0:T(8,128)(2,1)} %project.11.refs_0_), channel_id=1, source_target_pairs={{0,4},{1,5},{2,6},{3,7},{4,8},{5,9},{6,10},{7,11},{8,12},{9,13},{1... | collective-permute-start | bytes 393224 | tf_op jit(solution)/shard_map/ppermute | solution.py:95
  52.1 9.0 %collective-permute-start.16 = (bf16[128,512]{1,0:T(8,128)(2,1)}, bf16[128,512]{1,0:T(8,128)(2,1)S(1)}, u32[]{:S(2)}, u32[]{:S(2)}) collective-permute-start(bf16[128,512]{1,0:T(8,128)(2,1)} %project.11.refs_0_), channel_id=1, source_target_pairs={{0,12},{1,13},{2,14},{3,15},{4,0},{5,1},{6,2},{7,3},{8,4},{9,5},{1... | collective-permute-start | bytes 393224 | tf_op jit(solution)/shard_map/ppermute | solution.py:95
  55.0 8.8 %collective-permute-start.29 = (bf16[128,512]{1,0:T(8,128)(2,1)}, bf16[128,512]{1,0:T(8,128)(2,1)S(1)}, u32[]{:S(2)}, u32[]{:S(2)}) collective-permute-start(bf16[128,512]{1,0:T(8,128)(2,1)} %project.11.refs_0_), channel_id=1, source_target_pairs={{0,1},{1,0},{2,3},{3,2},{4,5},{5,4},{6,7},{7,6},{8,9},{9,8},{10,11... | collective-permute-start | bytes 393224 | tf_op jit(solution)/shard_map/ppermute | solution.py:95
  56.8 7.0 %collective-permute-start.28 = (bf16[128,512]{1,0:T(8,128)(2,1)S(1)}, bf16[128,512]{1,0:T(8,128)(2,1)S(1)}, u32[]{:S(2)}, u32[]{:S(2)}) collective-permute-start(bf16[128,512]{1,0:T(8,128)(2,1)S(1)} %collective-permute-done.27.refs_0_), channel_id=1, source_target_pairs={{0,1},{1,0},{2,3},{3,2},{4,5},{5,4},{6,7},{7,6},{8,9},{9,8},{10,11... | collective-permute-start | bytes 393224 | tf_op jit(solution)/shard_map/ppermute | solution.py:95
  59.6 8.4 %collective-permute-start.21 = (bf16[128,512]{1,0:T(8,128)(2,1)S(1)}, bf16[128,512]{1,0:T(8,128)(2,1)S(1)}, u32[]{:S(2)}, u32[]{:S(2)}) collective-permute-start(bf16[128,512]{1,0:T(8,128)(2,1)S(1)} %collective-permute-done.15.refs_0_), channel_id=1, source_target_pairs={{0,2},{1,3},{2,0},{3,1},{4,6},{5,7},{6,4},{7,5},{8,10},{9,11},{10,... | collective-permute-start | bytes 393224 | tf_op jit(solution)/shard_map/ppermute | solution.py:95
  61.1 7.0 %collective-permute-start.23 = (bf16[128,512]{1,0:T(8,128)(2,1)S(1)}, bf16[128,512]{1,0:T(8,128)(2,1)S(1)}, u32[]{:S(2)}, u32[]{:S(2)}) collective-permute-start(bf16[128,512]{1,0:T(8,128)(2,1)S(1)} %collective-permute-done.16.refs_2_), channel_id=1, source_target_pairs={{0,2},{1,3},{2,0},{3,1},{4,6},{5,7},{6,4},{7,5},{8,10},{9,11},{10,... | collective-permute-start | bytes 393224 | tf_op jit(solution)/shard_map/ppermute | solution.py:95
  62.0 8.0 %collective-permute-start.17 = (bf16[128,512]{1,0:T(8,128)(2,1)}, bf16[128,512]{1,0:T(8,128)(2,1)S(1)}, u32[]{:S(2)}, u32[]{:S(2)}) collective-permute-start(bf16[128,512]{1,0:T(8,128)(2,1)} %project.11.refs_0_), channel_id=1, source_target_pairs={{0,8},{1,9},{2,10},{3,11},{4,12},{5,13},{6,14},{7,15},{8,0},{9,1},... | collective-permute-start | bytes 393224 | tf_op jit(solution)/shard_map/ppermute | solution.py:95
  63.8 9.6 %collective-permute-start.25 = (bf16[128,512]{1,0:T(8,128)(2,1)S(1)}, bf16[128,512]{1,0:T(8,128)(2,1)S(1)}, u32[]{:S(2)}, u32[]{:S(2)}) collective-permute-start(bf16[128,512]{1,0:T(8,128)(2,1)S(1)} %collective-permute-done.15.refs_0_), channel_id=1, source_target_pairs={{0,1},{1,0},{2,3},{3,2},{4,5},{5,4},{6,7},{7,6},{8,9},{9,8},{10,11... | collective-permute-start | bytes 393224 | tf_op jit(solution)/shard_map/ppermute | solution.py:95
  63.8 9.7 %collective-permute-start.26 = (bf16[128,512]{1,0:T(8,128)(2,1)S(1)}, bf16[128,512]{1,0:T(8,128)(2,1)S(1)}, u32[]{:S(2)}, u32[]{:S(2)}) collective-permute-start(bf16[128,512]{1,0:T(8,128)(2,1)S(1)} %collective-permute-done.16.refs_2_), channel_id=1, source_target_pairs={{0,1},{1,0},{2,3},{3,2},{4,5},{5,4},{6,7},{7,6},{8,9},{9,8},{10,11... | collective-permute-start | bytes 393224 | tf_op jit(solution)/shard_map/ppermute | solution.py:95
  64.3 0.9 %copy-start.5 = (bf16[128,512]{1,0:T(8,128)(2,1)S(1)}, bf16[128,512]{1,0:T(8,128)(2,1)}, u32[]{:S(2)}) copy-start(bf16[128,512]{1,0:T(8,128)(2,1)} %project.11.refs_0_) | copy-start | bytes 393220
  68.0 10.6 %collective-permute-start.22 = (bf16[128,512]{1,0:T(8,128)(2,1)S(1)}, bf16[128,512]{1,0:T(8,128)(2,1)S(1)}, u32[]{:S(2)}, u32[]{:S(2)}) collective-permute-start(bf16[128,512]{1,0:T(8,128)(2,1)S(1)} %collective-permute-done.21.refs_0_), channel_id=1, source_target_pairs={{0,1},{1,0},{2,3},{3,2},{4,5},{5,4},{6,7},{7,6},{8,9},{9,8},{10,11... | collective-permute-start | bytes 393224 | tf_op jit(solution)/shard_map/ppermute | solution.py:95
  68.1 10.5 %collective-permute-start.24 = (bf16[128,512]{1,0:T(8,128)(2,1)S(1)}, bf16[128,512]{1,0:T(8,128)(2,1)S(1)}, u32[]{:S(2)}, u32[]{:S(2)}) collective-permute-start(bf16[128,512]{1,0:T(8,128)(2,1)S(1)} %collective-permute-done.23.refs_2_), channel_id=1, source_target_pairs={{0,1},{1,0},{2,3},{3,2},{4,5},{5,4},{6,7},{7,6},{8,9},{9,8},{10,11... | collective-permute-start | bytes 393224 | tf_op jit(solution)/shard_map/ppermute | solution.py:95
  70.0 8.1 %collective-permute-start.18 = (bf16[128,512]{1,0:T(8,128)(2,1)S(1)}, bf16[128,512]{1,0:T(8,128)(2,1)S(1)}, u32[]{:S(2)}, u32[]{:S(2)}) collective-permute-start(bf16[128,512]{1,0:T(8,128)(2,1)S(1)} %collective-permute-done.17.refs_0_), channel_id=1, source_target_pairs={{0,2},{1,3},{2,0},{3,1},{4,6},{5,7},{6,4},{7,5},{8,10},{9,11},{10,... | collective-permute-start | bytes 393224 | tf_op jit(solution)/shard_map/ppermute | solution.py:95
  73.4 9.9 %collective-permute-start.20 = (bf16[128,512]{1,0:T(8,128)(2,1)S(1)}, bf16[128,512]{1,0:T(8,128)(2,1)S(1)}, u32[]{:S(2)}, u32[]{:S(2)}) collective-permute-start(bf16[128,512]{1,0:T(8,128)(2,1)S(1)} %collective-permute-done.17.refs_0_), channel_id=1, source_target_pairs={{0,1},{1,0},{2,3},{3,2},{4,5},{5,4},{6,7},{7,6},{8,9},{9,8},{10,11... | collective-permute-start | bytes 393224 | tf_op jit(solution)/shard_map/ppermute | solution.py:95
  78.1 8.0 %collective-permute-start.19 = (bf16[128,512]{1,0:T(8,128)(2,1)S(1)}, bf16[128,512]{1,0:T(8,128)(2,1)S(1)}, u32[]{:S(2)}, u32[]{:S(2)}) collective-permute-start(bf16[128,512]{1,0:T(8,128)(2,1)S(1)} %collective-permute-done.18.refs_0_), channel_id=1, source_target_pairs={{0,1},{1,0},{2,3},{3,2},{4,5},{5,4},{6,7},{7,6},{8,9},{9,8},{10,11... | collective-permute-start | bytes 393224 | tf_op jit(solution)/shard_map/ppermute | solution.py:95
